TPU v7x, 32 devices: a whole 2x2x4 slice. The times are simulated.
32 devices in a mesh: cfg: 2 (over y), src: 4 (over z), col: 2 (over x), half: 2 (over core).
Axes of the slice: x: 2, y: 2, z: 4, core: 2. Of those that a mesh axis runs over, the one named last changes fastest.
Arguments:
- perambulator: bfloat16 [8, 4, 2, 512, 512], P(('cfg', 'src'), None, None, ('col', 'half')), parts along dimension 0, may hold values from -0.25 to 0.25
- elemental: bfloat16 [1, 8, 2, 128, 128], P(None, ('cfg', 'src')), parts along dimension 1, may hold values from -0.5 to 0.5
- source_order: int32 [8], P('cfg'), parts along dimension 0, may hold values from 0 to 3, as said below
- column_order: int32 [8, 128], P(('cfg', 'src')), parts along dimension 0, may hold values from 0 to 127, each once within a row
Outputs:
- meson_matrix: float32 [8, 2, 1, 1, 4], P(('cfg', 'src')), parts along dimension 0
There are 2 independent parts, one for each index of `cfg`. A program takes and returns all parts, laid end to end along the dimension named above; each array names one. Nothing has to cross between parts.
Inputs may be any that keep to these rules, and one draw needn't show every extreme that they name: `source_order`: each of 0 to 3 appears once. `column_order`: each row holds each of 0 to 127 once.
All inputs are finite; a program needn't handle non-finite values.
Results may differ from a plain program's by a relative error of at most 0.0042.
Values may be sent and summed in bfloat16 or wider, within the bound.
A program may use at most 128 MiB of HBM per device.

v0:
```python
import functools

import jax
import jax.numpy as jnp
from jax import lax
from jax.experimental import pallas as pl
from jax.experimental.pallas import tpu as pltpu
from jax.sharding import PartitionSpec as P

spin_sign = (1.0, 1.0, -1.0, -1.0)
MESH = pl.DeviceIdType.MESH
NT = (((1,), (1,)), ((), ()))


def dot_nt(a, b):
    return lax.dot_general(a, b, NT, preferred_element_type=jnp.float32)


def sends(source, target):
    even = lax.rem(source + target, 2) == 0
    return jnp.logical_and(even, source < target) | jnp.logical_and(
        jnp.logical_not(even), source > target
    )


def kernel(
    sizes,
    tiles_hbm, elem_hbm, order_hbm, column_hbm,
    out_ref,
    tiles, elem, order, column,
    sorted_tiles, coef, mirror, result,
    load_sem, tile_send, tile_recv, coef_send, coef_recv, share_send, share_recv,
    result_send, result_recv,
):
    src_count, col_count, half_count = sizes
    blocks = col_count * half_count
    block_cols, components = tiles.shape[2], tiles.shape[3]
    eigen = elem.shape[-1]
    spins = components // eigen
    piece = eigen // blocks
    p = lax.axis_index("src")
    b = lax.axis_index("col") * half_count + lax.axis_index("half")

    def device(slot, block):
        return {
            "src": slot,
            "col": lax.div(block, half_count),
            "half": lax.rem(block, half_count),
        }

    def wait_bytes(ref, sem):
        pltpu.make_async_copy(ref, ref, sem).wait()

    barrier = pltpu.get_barrier_semaphore()
    count = src_count * blocks
    me = p * blocks + b

    @pl.loop(1, count, unroll=count <= 16)
    def _(step):
        other = lax.rem(me + step, count)
        pl.semaphore_signal(
            barrier,
            inc=1,
            device_id=device(lax.div(other, blocks), lax.rem(other, blocks)),
            device_id_type=MESH,
        )

    loads = [
        pltpu.make_async_copy(order_hbm, order, load_sem.at[0]),
        pltpu.make_async_copy(tiles_hbm.at[0], tiles, load_sem.at[1]),
        pltpu.make_async_copy(elem_hbm.at[0, 0], elem, load_sem.at[2]),
        pltpu.make_async_copy(column_hbm, column, load_sem.at[3]),
    ]
    for load in loads:
        load.start()

    loads[2].wait()
    loads[3].wait()
    pick = (
        lax.broadcasted_iota(jnp.int32, (eigen, eigen), 0) == column[...]
    ).astype(jnp.float32).T.astype(jnp.bfloat16)
    both = jnp.concatenate([elem[0], elem[1]], axis=1)
    rows = jnp.dot(pick, both, preferred_element_type=jnp.float32).astype(jnp.bfloat16)
    coef[p, 0] = rows[:, :eigen]
    coef[p, 1] = rows[:, eigen:]

    loads[0].wait()
    loads[1].wait()

    @pl.loop(0, src_count)
    def _(slot):
        sorted_tiles[slot] = tiles[order[slot]]

    my_spin = lax.div(b * block_cols, eigen)
    my_lanes = pl.ds(pl.multiple_of(my_spin * eigen, eigen), eigen)
    my_rows = pl.ds(pl.multiple_of(b * block_cols, block_cols), block_cols)
    mirror[p, :, my_rows, :] = sorted_tiles[p, :, :, my_lanes]

    pl.semaphore_wait(barrier, count - 1)

    def partner(step):
        distance = 1 + lax.div(step, 2)
        slot = jnp.where(lax.rem(step, 2) == 0, p + distance, p - distance)
        valid = jnp.logical_and(slot >= 0, slot < src_count)
        return jnp.clip(slot, 0, src_count - 1), valid

    my_piece = pl.ds(pl.multiple_of(b * piece, piece), piece)

    def send_tile(slot, block):
        lanes = pl.ds(pl.multiple_of(lax.div(block * block_cols, eigen) * eigen, eigen), eigen)
        pltpu.make_async_remote_copy(
            src_ref=sorted_tiles.at[slot, :, :, lanes],
            dst_ref=mirror.at[p, :, my_rows, :],
            send_sem=tile_send.at[slot],
            recv_sem=tile_recv.at[p],
            device_id=device(slot, block),
            device_id_type=MESH,
        ).start()

    steps = 2 * (src_count - 1)

    @pl.loop(0, steps)
    def _(step):
        slot, valid = partner(step)

        @pl.when(jnp.logical_and(valid, sends(p, slot)))
        def _():
            pltpu.make_async_remote_copy(
                src_ref=coef.at[p, :, my_piece, :],
                dst_ref=coef.at[p, :, my_piece, :],
                send_sem=coef_send.at[slot],
                recv_sem=coef_recv.at[p],
                device_id={"src": slot},
                device_id_type=MESH,
            ).start()

    @pl.loop(0, steps)
    def _(step):
        slot, valid = partner(step)

        @pl.when(jnp.logical_and(valid, sends(p, slot)))
        def _():
            @pl.loop(0, blocks)
            def _(k):
                send_tile(slot, lax.rem(b + k, blocks))

    @pl.loop(1, blocks)
    def _(k):
        send_tile(p, lax.rem(b + k, blocks))

    @pl.loop(0, steps)
    def _(step):
        slot, valid = partner(step)

        @pl.when(jnp.logical_and(valid, sends(slot, p)))
        def _():
            wait_bytes(coef.at[slot, :, pl.ds(0, piece), :], coef_recv.at[slot])

            @pl.loop(1, blocks)
            def _(k):
                pltpu.make_async_remote_copy(
                    src_ref=coef.at[slot, :, my_piece, :],
                    dst_ref=coef.at[slot, :, my_piece, :],
                    send_sem=share_send.at[slot],
                    recv_sem=share_recv.at[slot],
                    device_id=device(p, lax.rem(b + k, blocks)),
                    device_id_type=MESH,
                ).start()

    def fold(value):
        return jnp.sum(value.reshape(block_cols // 8, 8, eigen), axis=0)

    offset = pl.ds(pl.multiple_of(lax.rem(b * block_cols, eigen), block_cols), block_cols)
    own_sign = jnp.where(my_spin < 2, spin_sign[0], spin_sign[2]).astype(jnp.float32)

    def pair(slot):
        own_real, own_imag = coef[p, 0, offset, :], coef[p, 1, offset, :]
        left = jnp.concatenate(
            [
                jnp.concatenate([own_real, -own_imag], axis=1),
                jnp.concatenate([own_imag, own_real], axis=1),
            ],
            axis=0,
        )
        far_real, far_imag = coef[slot, 0], coef[slot, 1]
        right = jnp.concatenate(
            [
                jnp.concatenate([far_real, -far_imag], axis=1),
                jnp.concatenate([far_imag, far_real], axis=1),
            ],
            axis=0,
        )
        total_real = jnp.zeros((8, eigen), jnp.float32)
        total_imag = jnp.zeros((8, eigen), jnp.float32)
        for spin in range(spins):
            part = slice(spin * eigen, (spin + 1) * eigen)
            near = jnp.concatenate(
                [sorted_tiles[slot, 0, :, part], sorted_tiles[slot, 1, :, part]], axis=1
            )
            away = jnp.concatenate([mirror[slot, 0, part, :], mirror[slot, 1, part, :]], axis=1)
            forward = dot_nt(near, right).astype(jnp.bfloat16).astype(jnp.float32)
            backward = dot_nt(left, away).astype(jnp.bfloat16).astype(jnp.float32)
            fr, fi = forward[:, :eigen], forward[:, eigen:]
            br, bi = backward[:block_cols], backward[block_cols:]
            total_real += spin_sign[spin] * fold(fr * br - fi * bi)
            total_imag += spin_sign[spin] * fold(fr * bi + fi * br)
        result[slot, b, 0] = own_sign * total_real
        result[slot, b, 1] = own_sign * total_imag

    def send_result(slot, target, block, there):
        pltpu.make_async_remote_copy(
            src_ref=result.at[slot, b],
            dst_ref=result.at[there, b],
            send_sem=result_send.at[slot],
            recv_sem=result_recv.at[there],
            device_id=device(target, block),
            device_id_type=MESH,
        ).start()

    def share_in_slot(slot):
        @pl.loop(1, blocks)
        def _(k):
            send_result(slot, p, lax.rem(b + k, blocks), slot)

    wait_bytes(mirror.at[p, :, pl.ds(0, components - block_cols), :], tile_recv.at[p])
    pair(p)
    share_in_slot(p)

    @pl.loop(0, steps)
    def _(step):
        slot, valid = partner(step)

        @pl.when(jnp.logical_and(valid, sends(slot, p)))
        def _():
            wait_bytes(coef.at[slot, :, pl.ds(0, eigen - piece), :], share_recv.at[slot])
            wait_bytes(mirror.at[slot], tile_recv.at[slot])
            pair(slot)

            @pl.loop(0, blocks)
            def _(k):
                send_result(slot, slot, lax.rem(b + k, blocks), p)

            share_in_slot(slot)

    wait_bytes(mirror.at[p, :, pl.ds(0, components - block_cols), :], tile_send.at[p])
    wait_bytes(result.at[p, pl.ds(0, blocks - 1)], result_send.at[p])

    @pl.loop(0, steps)
    def _(step):
        slot, valid = partner(step)

        @pl.when(jnp.logical_and(valid, sends(p, slot)))
        def _():
            wait_bytes(coef.at[slot, :, pl.ds(0, piece), :], coef_send.at[slot])
            wait_bytes(mirror.at[slot], tile_send.at[slot])

        @pl.when(jnp.logical_and(valid, sends(slot, p)))
        def _():
            wait_bytes(coef.at[slot, :, pl.ds(0, eigen - piece), :], share_send.at[slot])
            wait_bytes(result.at[slot], result_send.at[slot])
            wait_bytes(result.at[slot, pl.ds(0, blocks - 1)], result_send.at[slot])

    @pl.loop(0, src_count)
    def _(slot):
        here = jnp.logical_or(slot == p, sends(slot, p))

        @pl.when(here)
        def _():
            wait_bytes(result.at[slot, pl.ds(0, blocks - 1)], result_recv.at[slot])

        @pl.when(jnp.logical_not(here))
        def _():
            wait_bytes(result.at[slot], result_recv.at[slot])

    lane = lax.broadcasted_iota(jnp.int32, (1, src_count), 1)
    rows = [jnp.zeros((1, src_count), jnp.float32)] * 2
    for slot in range(src_count):
        total = jnp.sum(result[slot], axis=0)
        for part in (0, 1):
            rows[part] = jnp.where(lane == slot, jnp.sum(total[part], keepdims=True), rows[part])
    out_ref[0, 0, 0] = rows[0]
    out_ref[0, 1, 0] = rows[1]


def on_device(sizes, perambulator, elemental, source_order, column_order):
    operators = elemental.shape[0]
    eigen = elemental.shape[-1]
    _, slots, _, block_cols, components = perambulator.shape
    src_count, col_count, half_count = sizes
    blocks = col_count * half_count
    sem = pltpu.SemaphoreType.DMA
    return pl.pallas_call(
        functools.partial(kernel, sizes),
        out_shape=pltpu.VMEM((1, 2, operators, operators, slots), jnp.float32),
        in_specs=[pl.BlockSpec(memory_space=pl.ANY)] * 4,
        out_specs=pl.BlockSpec(memory_space=pltpu.VMEM),
        scratch_shapes=[
            pltpu.VMEM((slots, 2, block_cols, components), jnp.bfloat16),
            pltpu.VMEM((2, eigen, eigen), jnp.bfloat16),
            pltpu.SMEM((slots,), jnp.int32),
            pltpu.VMEM((1, eigen), jnp.int32),
            pltpu.VMEM((slots, 2, block_cols, components), jnp.bfloat16),
            pltpu.VMEM((slots, 2, eigen, eigen), jnp.bfloat16),
            pltpu.VMEM((slots, 2, components, eigen), jnp.bfloat16),
            pltpu.VMEM((slots, blocks, 2, 8, eigen), jnp.float32),
            sem((4,)),
        ]
        + [sem((slots,))] * 8,
        compiler_params=pltpu.CompilerParams(collective_id=0, has_side_effects=True),
    )(perambulator, elemental, source_order, column_order)


def solution(mesh):
    sizes = (mesh.shape["src"], mesh.shape["col"], mesh.shape["half"])
    return jax.shard_map(
        functools.partial(on_device, sizes),
        mesh=mesh,
        in_specs=(
            P(("cfg", "src"), None, None, ("col", "half"), None),
            P(None, ("cfg", "src"), None, None, None),
            P("cfg"),
            P(("cfg", "src"), None),
        ),
        out_specs=P(("cfg", "src"), None, None, None, None),
        check_vma=False,
    )
```

profile of v0, /device:TPU:0, one launch (start us, length us, event | category | flops | bytes accessed | tf_op | source)
XLA Modules:
  0.0 23.4 jit_solution(10208025240795799431)
XLA Ops:
  0.0 22.9 %shard_map.46 = f32[1,2,1,1,4]{4,3,2,1,0:T(1,128)S(1)} custom-call(bf16[1,4,2,128,512]{4,3,2,1,0:T(8,128)(2,1)} %tiles_hbm.1, bf16[1,1,2,128,128]{4,3,2,1,0:T(8,128)(2,1)} %elem_hbm.1, s32[4]{0:T(128)} %order_hbm.1, s32[1,128]{1,0:T(1,128)} %column_hbm.1), custom_call_target="tpu_custom_call" | custom-call | tf_op jit(solution)/shard_map/pallas_call | solution.py:292
  22.9 0.6 %copy.6 = f32[1,2,1,1,4]{4,3,2,1,0:T(1,128)} copy(f32[1,2,1,1,4]{4,3,2,1,0:T(1,128)S(1)} %shard_map.46) | data formatting | bytes 64
where the time goes:
time: 23.6 us; the launch traced here: 23.4 us
  Pallas kernels  22.9 us (97%)
  local copies, waits for them, and re-layouts  0.56 us (2%)
    pallas_call x1, Pallas kernels, on_device(): pl.pallas_call(functools.partial(kernel, sizes), out_shape=pltpu.VMEM((1,...  22.9 us
    unnamed x1, local copies, waits for them, and re-layouts  0.56 us

commit v1 on v0

--- a/solution.py
+++ b/solution.py
@@ -30,7 +30,7 @@
     tiles, elem, order, column,
     sorted_tiles, coef, mirror, result,
     load_sem, tile_send, tile_recv, coef_send, coef_recv, share_send, share_recv,
-    result_send, result_recv,
+    result_send, result_recv, above, below,
 ):
     src_count, col_count, half_count = sizes
     blocks = col_count * half_count
@@ -52,18 +52,16 @@
         pltpu.make_async_copy(ref, ref, sem).wait()
 
     barrier = pltpu.get_barrier_semaphore()
-    count = src_count * blocks
-    me = p * blocks + b
-
-    @pl.loop(1, count, unroll=count <= 16)
-    def _(step):
-        other = lax.rem(me + step, count)
+
+    def signal(sem, slot, block):
         pl.semaphore_signal(
-            barrier,
-            inc=1,
-            device_id=device(lax.div(other, blocks), lax.rem(other, blocks)),
-            device_id_type=MESH,
+            sem, inc=1, device_id=device(slot, block), device_id_type=MESH
         )
+
+    @pl.when(p < src_count - 1)
+    def _():
+        for k in range(blocks):
+            signal(barrier, p + 1, k)
 
     loads = [
         pltpu.make_async_copy(order_hbm, order, load_sem.at[0]),
@@ -73,6 +71,40 @@
     ]
     for load in loads:
         load.start()
+
+    @pl.when(p > 0)
+    def _():
+        pl.semaphore_wait(barrier, blocks)
+        for k in range(blocks):
+            signal(above.at[p], p - 1, k)
+
+    @pl.when(p < src_count - 1)
+    def _():
+        pl.semaphore_wait(above.at[p + 1], blocks)
+
+        @pl.when(p > 0)
+        def _():
+            signal(above.at[p + 1], p - 1, b)
+
+    @pl.when(p > 0)
+    def _():
+        @pl.when(p > 1)
+        def _():
+            pl.semaphore_wait(below, 1)
+
+    @pl.when(jnp.logical_and(p > 0, p < src_count - 1))
+    def _():
+        signal(below, p + 1, b)
+
+    @pl.loop(0, src_count)
+    def _(slot):
+        @pl.when(slot > p + 1)
+        def _():
+            pl.semaphore_wait(above.at[slot], 1)
+
+            @pl.when(p > 0)
+            def _():
+                signal(above.at[slot], p - 1, b)
 
     loads[2].wait()
     loads[3].wait()
@@ -95,8 +127,6 @@
     my_lanes = pl.ds(pl.multiple_of(my_spin * eigen, eigen), eigen)
     my_rows = pl.ds(pl.multiple_of(b * block_cols, block_cols), block_cols)
     mirror[p, :, my_rows, :] = sorted_tiles[p, :, :, my_lanes]
-
-    pl.semaphore_wait(barrier, count - 1)
 
     def partner(step):
         distance = 1 + lax.div(step, 2)
@@ -305,7 +335,8 @@
             pltpu.VMEM((slots, blocks, 2, 8, eigen), jnp.float32),
             sem((4,)),
         ]
-        + [sem((slots,))] * 8,
+        + [sem((slots,))] * 8
+        + [pltpu.SemaphoreType.REGULAR((slots,)), pltpu.SemaphoreType.REGULAR],
         compiler_params=pltpu.CompilerParams(collective_id=0, has_side_effects=True),
     )(perambulator, elemental, source_order, column_order)
 

time: 23.6 us -> 25.7 us (1.089)
  Pallas kernels: 22.9 us -> 25 us
    pallas_call x1, Pallas kernels: 22.9 us -> 25 us  [on_device(): pl.pallas_call(functools.partial(kernel, sizes), out_shape=pltpu.VMEM((1,...]
where the time goes in v1:
time: 25.7 us; the launch traced here: 25.6 us
  Pallas kernels  25 us (97%)
  local copies, waits for them, and re-layouts  0.56 us (2%)
    pallas_call x1, Pallas kernels, on_device(): pl.pallas_call(functools.partial(kernel, sizes), out_shape=pltpu.VMEM((1,...  25 us
    unnamed x1, local copies, waits for them, and re-layouts  0.56 us

profile of v1, /device:TPU:0, one launch (start us, length us, event | category | flops | bytes accessed | tf_op | source)
XLA Modules:
  0.0 25.6 jit_solution(17903864714483458374)
XLA Ops:
  0.0 25.0 %shard_map.46 = f32[1,2,1,1,4]{4,3,2,1,0:T(1,128)S(1)} custom-call(bf16[1,4,2,128,512]{4,3,2,1,0:T(8,128)(2,1)} %tiles_hbm.1, bf16[1,1,2,128,128]{4,3,2,1,0:T(8,128)(2,1)} %elem_hbm.1, s32[4]{0:T(128)} %order_hbm.1, s32[1,128]{1,0:T(1,128)} %column_hbm.1), custom_call_target="tpu_custom_call" | custom-call | tf_op jit(solution)/shard_map/pallas_call | solution.py:322
  25.0 0.6 %copy.6 = f32[1,2,1,1,4]{4,3,2,1,0:T(1,128)} copy(f32[1,2,1,1,4]{4,3,2,1,0:T(1,128)S(1)} %shard_map.46) | data formatting | bytes 64

commit v2 on v1

v2 whole, which is shorter than its diff:
```python
import functools

import jax
import jax.numpy as jnp
from jax import lax
from jax.experimental import pallas as pl
from jax.experimental.pallas import tpu as pltpu
from jax.sharding import PartitionSpec as P

spin_sign = (1.0, 1.0, -1.0, -1.0)
MESH = pl.DeviceIdType.MESH
NT = (((1,), (1,)), ((), ()))


def dot_nt(a, b):
    return lax.dot_general(a, b, NT, preferred_element_type=jnp.float32)


def kernel(
    sizes,
    tiles_hbm, elem_hbm, order_hbm, column_hbm,
    out_ref,
    tiles, elem, order, column,
    near, coef, left, mirror, forward, partial, result, total,
    load_sem, tile_send, tile_recv, coef_send, coef_recv, share_send, share_recv,
    diag_send, diag_recv, result_send, result_recv, above, below,
):
    src_count, col_count, half_count = sizes
    blocks = col_count * half_count
    half = blocks // 2
    block_cols, components = tiles.shape[2], tiles.shape[3]
    eigen = elem.shape[-1]
    spins = components // eigen
    piece = eigen // blocks
    last = src_count - 1
    p = lax.axis_index("src")
    b = lax.axis_index("col") * half_count + lax.axis_index("half")
    offsets = [2 * j if j < half else 2 * (j - half) + 1 for j in range(blocks)]
    each = functools.partial(pl.loop, unroll=src_count <= 8)

    def device(slot, block):
        return {
            "src": slot,
            "col": lax.div(block, half_count),
            "half": lax.rem(block, half_count),
        }

    def signal(sem, slot, block):
        pl.semaphore_signal(sem, inc=1, device_id=device(slot, block), device_id_type=MESH)

    def send(src, dst, send_sem, recv_sem, slot, block):
        pltpu.make_async_remote_copy(
            src_ref=src, dst_ref=dst, send_sem=send_sem, recv_sem=recv_sem,
            device_id=device(slot, block), device_id_type=MESH,
        ).start()

    def wait_bytes(ref, sem):
        pltpu.make_async_copy(ref, ref, sem).wait()

    def shifted(block, offset):
        return lax.rem(block + offset + blocks, blocks)

    def spin_of(block):
        return lax.div(block * block_cols, eigen)

    def sign_of(block):
        return jnp.where(spin_of(block) < 2, spin_sign[0], spin_sign[2]).astype(jnp.float32)

    def rows_of(block):
        return pl.ds(pl.multiple_of(lax.rem(block * block_cols, eigen), block_cols), block_cols)

    def upward(low, high):
        distance = high - low
        whole = jnp.where(lax.rem(distance, 2) == 0, blocks, 0)
        return jnp.where(jnp.logical_and(low == 0, distance > 1), whole, half)

    def count(source, target):
        n = upward(jnp.minimum(source, target), jnp.maximum(source, target))
        return jnp.where(source < target, n, blocks - n)

    def goes(source, target, j):
        n = upward(jnp.minimum(source, target), jnp.maximum(source, target))
        return jnp.where(source < target, j < n, j >= n)

    barrier = pltpu.get_barrier_semaphore()

    @pl.when(p < last)
    def _():
        for k in range(blocks):
            signal(barrier, p + 1, k)

    loads = [
        pltpu.make_async_copy(elem_hbm.at[0, 0], elem, load_sem.at[0]),
        pltpu.make_async_copy(column_hbm, column, load_sem.at[1]),
        pltpu.make_async_copy(order_hbm, order, load_sem.at[2]),
        pltpu.make_async_copy(tiles_hbm.at[0], tiles, load_sem.at[3]),
    ]
    for load in loads:
        load.start()

    @pl.when(p > 0)
    def _():
        pl.semaphore_wait(barrier, blocks)
        for k in range(blocks):
            signal(above.at[p], p - 1, k)

    loads[0].wait()
    loads[1].wait()
    pick = (
        lax.broadcasted_iota(jnp.int32, (eigen, eigen), 0) == column[...]
    ).astype(jnp.float32).T.astype(jnp.bfloat16)
    both = jnp.concatenate([elem[0], elem[1]], axis=1)
    picked = jnp.dot(pick, both, preferred_element_type=jnp.float32).astype(jnp.bfloat16)
    coef[p, 0] = picked[:, :eigen]
    coef[p, 1] = picked[:, eigen:]

    loads[2].wait()
    loads[3].wait()

    @each(0, src_count)
    def _(slot):
        for spin in range(spins):
            near[slot, spin] = tiles[order[slot], :, :, spin * eigen : (spin + 1) * eigen]

    my_piece = pl.ds(pl.multiple_of(b * piece, piece), piece)

    def send_coef(slot):
        @pl.when(count(p, slot) > 0)
        def _():
            send(
                coef.at[p, :, my_piece, :], coef.at[p, :, my_piece, :],
                coef_send.at[slot], coef_recv.at[p], slot, b,
            )

    def send_unit(slot, j):
        @pl.when(goes(p, slot, j))
        def _():
            block = jnp.where(p < slot, shifted(b, offsets[j]), shifted(b, -offsets[j]))
            send(
                near.at[slot, spin_of(block)], mirror.at[p, b],
                tile_send.at[slot], tile_recv.at[p, b], slot, block,
            )

    def send_far(slot):
        send_coef(slot)
        for j in range(blocks):
            send_unit(slot, j)

    @pl.when(p > 0)
    def _():
        send_coef(p - 1)
        send_unit(p - 1, half)

    @pl.when(p < last)
    def _():
        pl.semaphore_wait(above.at[p + 1], blocks)

        @pl.when(p > 0)
        def _():
            signal(above.at[p + 1], p - 1, b)

        @pl.when(p < 2)
        def _():
            signal(below, p + 1, b)

        send_coef(p + 1)
        send_unit(p + 1, 0)

    @each(0, src_count)
    def _(slot):
        @pl.when(slot > p + 1)
        def _():
            pl.semaphore_wait(above.at[slot], 1)

            @pl.when(p > 0)
            def _():
                signal(above.at[slot], p - 1, b)

            send_far(slot)

    @pl.when(p > 0)
    def _():
        pl.semaphore_wait(below, 1)

        @pl.when(jnp.logical_and(p > 1, p < last))
        def _():
            signal(below, p + 1, b)

    @each(0, src_count)
    def _(slot):
        @pl.when(slot < p - 1)
        def _():
            send_far(slot)

    @pl.when(p < last)
    def _():
        for j in range(1, half):
            send_unit(p + 1, j)

    @pl.when(p > 0)
    def _():
        for j in range(half + 1, blocks):
            send_unit(p - 1, j)

    def diag_source(k):
        return b >= half if k == half else b >= 0

    def diag_target(k):
        return b < half if k == half else b >= 0

    for k in range(1, half + 1):
        @pl.when(diag_source(k))
        def _():
            block = shifted(b, -k)
            send(
                near.at[p, spin_of(block)], mirror.at[p, b],
                diag_send.at[k], diag_recv.at[k], p, block,
            )

    own_real, own_imag = coef[p, 0, rows_of(b), :], coef[p, 1, rows_of(b), :]
    left[:block_cols, :eigen] = own_real
    left[:block_cols, eigen:] = -own_imag
    left[block_cols:, :eigen] = own_imag
    left[block_cols:, eigen:] = own_real

    def make_forward(slot, block):
        far_real, far_imag = coef[slot, 0, rows_of(block), :], coef[slot, 1, rows_of(block), :]
        mine = jnp.concatenate([near[slot, spin_of(block), 0], near[slot, spin_of(block), 1]], axis=1)
        real = jnp.concatenate([far_real, -far_imag], axis=1)
        imag = jnp.concatenate([far_imag, far_real], axis=1)
        forward[slot, block, 0] = dot_nt(mine, real).astype(jnp.bfloat16)
        forward[slot, block, 1] = dot_nt(mine, imag).astype(jnp.bfloat16)

    def fold(value):
        return jnp.sum(value.reshape(block_cols // 8, 8, block_cols), axis=0)

    def multiply(slot, block, away, weight, first):
        backward = dot_nt(left[...], jnp.concatenate([away[0], away[1]], axis=1))
        backward = backward.astype(jnp.bfloat16).astype(jnp.float32)
        br, bi = backward[:block_cols], backward[block_cols:]
        fr = forward[slot, block, 0].astype(jnp.float32)
        fi = forward[slot, block, 1].astype(jnp.float32)
        scale = weight * sign_of(block) * sign_of(b)
        real = scale * fold(fr * br - fi * bi)
        imag = scale * fold(fr * bi + fi * br)
        packed = jnp.concatenate([real[:4] + real[4:], imag[:4] + imag[4:]], axis=0)
        if first:
            partial[slot] = packed
        else:
            partial[slot] += packed

    def share_result(slot):
        result[slot, 0, b] = partial[slot]
        for k in range(1, blocks):
            block = shifted(b, k)
            send(
                result.at[slot, 0, b], result.at[slot, 0, b],
                result_send.at[slot], result_recv.at[slot, 0], p, block,
            )

    def send_result(slot):
        for k in range(blocks):
            block = shifted(b, k)
            send(
                result.at[slot, 0, b], result.at[p, 1, b],
                result_send.at[slot], result_recv.at[p, 1], slot, block,
            )

    @each(0, src_count)
    def _(slot):
        @pl.when(jnp.logical_and(slot != p, count(slot, p) > 0))
        def _():
            wait_bytes(coef.at[slot, :, pl.ds(0, piece), :], coef_recv.at[slot])
            for k in range(1, blocks):
                send(
                    coef.at[slot, :, my_piece, :], coef.at[slot, :, my_piece, :],
                    share_send.at[slot], share_recv.at[slot], p, shifted(b, k),
                )

    make_forward(p, b)
    multiply(p, b, near[p, spin_of(b)], 1.0, True)
    for k in range(1, half + 1):
        @pl.when(diag_target(k))
        def _():
            block = shifted(b, k)
            make_forward(p, block)
            wait_bytes(mirror.at[p, block], diag_recv.at[k])
            multiply(p, block, mirror[p, block], 2.0, False)
    share_result(p)

    def source_block(slot, j):
        return jnp.where(slot < p, shifted(b, -offsets[j]), shifted(b, offsets[j]))

    @each(0, src_count)
    def _(slot):
        @pl.when(jnp.logical_and(slot != p, count(slot, p) > 0))
        def _():
            wait_bytes(coef.at[slot, :, pl.ds(0, eigen - piece), :], share_recv.at[slot])
            partial[slot] = jnp.zeros(partial.shape[1:], jnp.float32)
            for j in range(blocks):
                @pl.when(goes(slot, p, j))
                def _():
                    make_forward(slot, source_block(slot, j))

    def take_unit(slot, j):
        @pl.when(goes(slot, p, j))
        def _():
            block = source_block(slot, j)
            wait_bytes(mirror.at[slot, block], tile_recv.at[slot, block])
            multiply(slot, block, mirror[slot, block], 1.0, False)

    def finish(slot):
        @pl.when(count(slot, p) > 0)
        def _():
            share_result(slot)
            send_result(slot)

    @pl.when(p > 0)
    def _():
        take_unit(p - 1, 0)

    @pl.when(p < last)
    def _():
        take_unit(p + 1, half)

    @each(0, src_count)
    def _(slot):
        @pl.when(jnp.logical_or(slot > p + 1, slot < p - 1))
        def _():
            for j in range(blocks):
                take_unit(slot, j)
            finish(slot)

    @pl.when(p > 0)
    def _():
        for j in range(1, half):
            take_unit(p - 1, j)
        finish(p - 1)

    @pl.when(p < last)
    def _():
        for j in range(half + 1, blocks):
            take_unit(p + 1, j)
        finish(p + 1)

    wait_bytes(result.at[p, 0, pl.ds(0, blocks - 1)], result_send.at[p])
    for k in range(1, half + 1):
        @pl.when(diag_source(k))
        def _():
            wait_bytes(mirror.at[p, 0], diag_send.at[k])

    @each(0, src_count)
    def _(slot):
        @pl.when(slot != p)
        def _():
            sent, received = count(p, slot), count(slot, p)

            @pl.when(sent > 0)
            def _():
                wait_bytes(coef.at[slot, :, pl.ds(0, piece), :], coef_send.at[slot])

            @pl.when(sent == half)
            def _():
                wait_bytes(mirror.at[slot, pl.ds(0, half)], tile_send.at[slot])

            @pl.when(sent == blocks)
            def _():
                wait_bytes(mirror.at[slot], tile_send.at[slot])

            @pl.when(received > 0)
            def _():
                wait_bytes(coef.at[slot, :, pl.ds(0, eigen - piece), :], share_send.at[slot])
                wait_bytes(result.at[slot, 0], result_send.at[slot])
                wait_bytes(result.at[slot, 0, pl.ds(0, blocks - 1)], result_send.at[slot])

    @each(0, src_count)
    def _(slot):
        total[slot] = jnp.zeros(total.shape[1:], jnp.float32)

        @pl.when(jnp.logical_or(slot == p, count(slot, p) > 0))
        def _():
            wait_bytes(result.at[slot, 0, pl.ds(0, blocks - 1)], result_recv.at[slot, 0])
            total[slot] += jnp.sum(result[slot, 0], axis=0)

        @pl.when(jnp.logical_and(slot != p, count(p, slot) > 0))
        def _():
            wait_bytes(result.at[slot, 1], result_recv.at[slot, 1])
            total[slot] += jnp.sum(result[slot, 1], axis=0)

    lane = lax.broadcasted_iota(jnp.int32, (1, src_count), 1)
    rows = [jnp.zeros((1, src_count), jnp.float32)] * 2
    for slot in range(src_count):
        for part in (0, 1):
            value = jnp.sum(total[slot, 4 * part : 4 * part + 4], keepdims=True)
            rows[part] = jnp.where(lane == slot, value, rows[part])
    out_ref[0, 0, 0] = rows[0]
    out_ref[0, 1, 0] = rows[1]


def on_device(sizes, perambulator, elemental, source_order, column_order):
    operators = elemental.shape[0]
    eigen = elemental.shape[-1]
    _, slots, _, block_cols, components = perambulator.shape
    src_count, col_count, half_count = sizes
    blocks = col_count * half_count
    spins = components // eigen
    sem = pltpu.SemaphoreType.DMA
    flag = pltpu.SemaphoreType.REGULAR
    return pl.pallas_call(
        functools.partial(kernel, sizes),
        out_shape=pltpu.VMEM((1, 2, operators, operators, slots), jnp.float32),
        in_specs=[pl.BlockSpec(memory_space=pl.ANY)] * 4,
        out_specs=pl.BlockSpec(memory_space=pltpu.VMEM),
        scratch_shapes=[
            pltpu.VMEM((slots, 2, block_cols, components), jnp.bfloat16),
            pltpu.VMEM((2, eigen, eigen), jnp.bfloat16),
            pltpu.SMEM((slots,), jnp.int32),
            pltpu.VMEM((1, eigen), jnp.int32),
            pltpu.VMEM((slots, spins, 2, block_cols, eigen), jnp.bfloat16),
            pltpu.VMEM((slots, 2, eigen, eigen), jnp.bfloat16),
            pltpu.VMEM((2 * block_cols, 2 * eigen), jnp.bfloat16),
            pltpu.VMEM((slots, blocks, 2, block_cols, eigen), jnp.bfloat16),
            pltpu.VMEM((slots, blocks, 2, block_cols, block_cols), jnp.bfloat16),
            pltpu.VMEM((slots, 8, block_cols), jnp.float32),
            pltpu.VMEM((slots, 2, blocks, 8, block_cols), jnp.float32),
            pltpu.VMEM((slots, 8, block_cols), jnp.float32),
            sem((4,)),
            sem((slots,)),
            sem((slots, blocks)),
            sem((slots,)),
            sem((slots,)),
            sem((slots,)),
            sem((slots,)),
            sem((blocks,)),
            sem((blocks,)),
            sem((slots,)),
            sem((slots, 2)),
            flag((slots,)),
            flag,
        ],
        compiler_params=pltpu.CompilerParams(collective_id=0, has_side_effects=True),
    )(perambulator, elemental, source_order, column_order)


def solution(mesh):
    sizes = (mesh.shape["src"], mesh.shape["col"], mesh.shape["half"])
    return jax.shard_map(
        functools.partial(on_device, sizes),
        mesh=mesh,
        in_specs=(
            P(("cfg", "src"), None, None, ("col", "half"), None),
            P(None, ("cfg", "src"), None, None, None),
            P("cfg"),
            P(("cfg", "src"), None),
        ),
        out_specs=P(("cfg", "src"), None, None, None, None),
        check_vma=False,
    )
```

time: 25.7 us -> 25.3 us (0.984)
  Pallas kernels: 25 us -> 24.6 us
    pallas_call x1, Pallas kernels: 25 us -> 24.6 us  [on_device(): pl.pallas_call(functools.partial(kernel, sizes), out_shape=pltpu.VMEM((1,...]
where the time goes in v2:
time: 25.3 us; the launch traced here: 25.2 us
  Pallas kernels  24.6 us (97%)
  local copies, waits for them, and re-layouts  0.56 us (2%)
    pallas_call x1, Pallas kernels, on_device(): pl.pallas_call(functools.partial(kernel, sizes), out_shape=pltpu.VMEM((1,...  24.6 us
    unnamed x1, local copies, waits for them, and re-layouts  0.56 us

profile of v2, /device:TPU:0, one launch (start us, length us, event | category | flops | bytes accessed | tf_op | source)
XLA Modules:
  0.0 25.2 jit_solution(7256553847766823221)
XLA Ops:
  0.0 24.6 %shard_map.46 = f32[1,2,1,1,4]{4,3,2,1,0:T(1,128)S(1)} custom-call(bf16[1,4,2,128,512]{4,3,2,1,0:T(8,128)(2,1)} %tiles_hbm.1, bf16[1,1,2,128,128]{4,3,2,1,0:T(8,128)(2,1)} %elem_hbm.1, s32[4]{0:T(128)} %order_hbm.1, s32[1,128]{1,0:T(1,128)} %column_hbm.1), custom_call_target="tpu_custom_call" | custom-call | tf_op jit(solution)/shard_map/pallas_call | solution.py:409
  24.6 0.6 %copy.6 = f32[1,2,1,1,4]{4,3,2,1,0:T(1,128)} copy(f32[1,2,1,1,4]{4,3,2,1,0:T(1,128)S(1)} %shard_map.46) | data formatting | bytes 64

commit v3 on v2

--- a/solution.py
+++ b/solution.py
@@ -23,7 +23,7 @@
     tiles, elem, order, column,
     near, coef, left, mirror, forward, partial, result, total,
     load_sem, tile_send, tile_recv, coef_send, coef_recv, share_send, share_recv,
-    diag_send, diag_recv, result_send, result_recv, above, below,
+    diag_send, diag_recv, result_send, result_recv, above,
 ):
     src_count, col_count, half_count = sizes
     blocks = col_count * half_count
@@ -61,18 +61,21 @@
         return lax.rem(block + offset + blocks, blocks)
 
     def spin_of(block):
+        if isinstance(block, int):
+            return block * block_cols // eigen
         return lax.div(block * block_cols, eigen)
 
     def sign_of(block):
         return jnp.where(spin_of(block) < 2, spin_sign[0], spin_sign[2]).astype(jnp.float32)
 
     def rows_of(block):
+        if isinstance(block, int):
+            return pl.ds(block * block_cols % eigen, block_cols)
         return pl.ds(pl.multiple_of(lax.rem(block * block_cols, eigen), block_cols), block_cols)
 
     def upward(low, high):
-        distance = high - low
-        whole = jnp.where(lax.rem(distance, 2) == 0, blocks, 0)
-        return jnp.where(jnp.logical_and(low == 0, distance > 1), whole, half)
+        whole = jnp.where(jnp.logical_or(lax.rem(high, 2) == 0, high - low == 1), blocks, 0)
+        return jnp.where(high == 1, half, whole)
 
     def count(source, target):
         n = upward(jnp.minimum(source, target), jnp.maximum(source, target))
@@ -84,10 +87,15 @@
 
     barrier = pltpu.get_barrier_semaphore()
 
-    @pl.when(p < last)
-    def _():
-        for k in range(blocks):
-            signal(barrier, p + 1, k)
+    for k in range(1, blocks):
+        signal(barrier, p, shifted(b, k))
+
+    @each(0, src_count)
+    def _(slot):
+        @pl.when(slot > p)
+        def _():
+            for k in range(blocks):
+                signal(barrier, slot, k)
 
     loads = [
         pltpu.make_async_copy(elem_hbm.at[0, 0], elem, load_sem.at[0]),
@@ -98,11 +106,13 @@
     for load in loads:
         load.start()
 
-    @pl.when(p > 0)
-    def _():
-        pl.semaphore_wait(barrier, blocks)
-        for k in range(blocks):
-            signal(above.at[p], p - 1, k)
+    pl.semaphore_wait(barrier, blocks - 1 + p * blocks)
+
+    @each(0, src_count)
+    def _(slot):
+        @pl.when(slot < p)
+        def _():
+            signal(above.at[p], slot, b)
 
     loads[0].wait()
     loads[1].wait()
@@ -135,72 +145,63 @@
     def send_unit(slot, j):
         @pl.when(goes(p, slot, j))
         def _():
-            block = jnp.where(p < slot, shifted(b, offsets[j]), shifted(b, -offsets[j]))
+            offset = jnp.where(lax.rem(b, 2) == 0, offsets[j], offsets[j ^ 1])
+            block = jnp.where(p < slot, shifted(b, offset), shifted(b, -offset))
             send(
                 near.at[slot, spin_of(block)], mirror.at[p, b],
                 tile_send.at[slot], tile_recv.at[p, b], slot, block,
             )
 
-    def send_far(slot):
-        send_coef(slot)
-        for j in range(blocks):
+    def send_units(slot, start, stop):
+        for j in range(start, stop):
             send_unit(slot, j)
 
-    @pl.when(p > 0)
-    def _():
-        send_coef(p - 1)
-        send_unit(p - 1, half)
+    @each(0, src_count)
+    def _(slot):
+        @pl.when(slot < p)
+        def _():
+            send_coef(slot)
+
+    @each(0, src_count)
+    def _(slot):
+        @pl.when(slot < p)
+        def _():
+            send_units(slot, 0, blocks)
 
     @pl.when(p < last)
     def _():
-        pl.semaphore_wait(above.at[p + 1], blocks)
-
-        @pl.when(p > 0)
-        def _():
-            signal(above.at[p + 1], p - 1, b)
-
-        @pl.when(p < 2)
-        def _():
-            signal(below, p + 1, b)
-
+        pl.semaphore_wait(above.at[p + 1], 1)
         send_coef(p + 1)
-        send_unit(p + 1, 0)
+        send_units(p + 1, 0, 1)
 
     @each(0, src_count)
     def _(slot):
         @pl.when(slot > p + 1)
         def _():
             pl.semaphore_wait(above.at[slot], 1)
-
-            @pl.when(p > 0)
-            def _():
-                signal(above.at[slot], p - 1, b)
-
-            send_far(slot)
-
-    @pl.when(p > 0)
-    def _():
-        pl.semaphore_wait(below, 1)
-
-        @pl.when(jnp.logical_and(p > 1, p < last))
-        def _():
-            signal(below, p + 1, b)
-
-    @each(0, src_count)
-    def _(slot):
-        @pl.when(slot < p - 1)
-        def _():
-            send_far(slot)
+            send_coef(slot)
+            send_units(slot, 0, blocks)
 
     @pl.when(p < last)
     def _():
-        for j in range(1, half):
-            send_unit(p + 1, j)
-
-    @pl.when(p > 0)
-    def _():
-        for j in range(half + 1, blocks):
-            send_unit(p - 1, j)
+        send_units(p + 1, 1, blocks)
+
+    def others(act):
+        @each(0, src_count)
+        def _(slot):
+            @pl.when(slot != p)
+            def _():
+                act(slot)
+
+    def share_coef(slot):
+        @pl.when(count(slot, p) > 0)
+        def _():
+            wait_bytes(coef.at[slot, :, pl.ds(0, piece), :], coef_recv.at[slot])
+            for k in range(1, blocks):
+                send(
+                    coef.at[slot, :, my_piece, :], coef.at[slot, :, my_piece, :],
+                    share_send.at[slot], share_recv.at[slot], p, shifted(b, k),
+                )
 
     def diag_source(k):
         return b >= half if k == half else b >= 0
@@ -228,16 +229,17 @@
         mine = jnp.concatenate([near[slot, spin_of(block), 0], near[slot, spin_of(block), 1]], axis=1)
         real = jnp.concatenate([far_real, -far_imag], axis=1)
         imag = jnp.concatenate([far_imag, far_real], axis=1)
-        forward[slot, block, 0] = dot_nt(mine, real).astype(jnp.bfloat16)
-        forward[slot, block, 1] = dot_nt(mine, imag).astype(jnp.bfloat16)
+        product = dot_nt(jnp.concatenate([real, imag], axis=0), mine).astype(jnp.bfloat16)
+        forward[slot, block, 0] = product[:block_cols]
+        forward[slot, block, 1] = product[block_cols:]
 
     def fold(value):
         return jnp.sum(value.reshape(block_cols // 8, 8, block_cols), axis=0)
 
     def multiply(slot, block, away, weight, first):
-        backward = dot_nt(left[...], jnp.concatenate([away[0], away[1]], axis=1))
+        backward = dot_nt(jnp.concatenate([away[0], away[1]], axis=1), left[...])
         backward = backward.astype(jnp.bfloat16).astype(jnp.float32)
-        br, bi = backward[:block_cols], backward[block_cols:]
+        br, bi = backward[:, :block_cols], backward[:, block_cols:]
         fr = forward[slot, block, 0].astype(jnp.float32)
         fi = forward[slot, block, 1].astype(jnp.float32)
         scale = weight * sign_of(block) * sign_of(b)
@@ -266,48 +268,55 @@
                 result_send.at[slot], result_recv.at[p, 1], slot, block,
             )
 
-    @each(0, src_count)
-    def _(slot):
-        @pl.when(jnp.logical_and(slot != p, count(slot, p) > 0))
-        def _():
-            wait_bytes(coef.at[slot, :, pl.ds(0, piece), :], coef_recv.at[slot])
-            for k in range(1, blocks):
-                send(
-                    coef.at[slot, :, my_piece, :], coef.at[slot, :, my_piece, :],
-                    share_send.at[slot], share_recv.at[slot], p, shifted(b, k),
-                )
-
     make_forward(p, b)
     multiply(p, b, near[p, spin_of(b)], 1.0, True)
     for k in range(1, half + 1):
         @pl.when(diag_target(k))
         def _():
-            block = shifted(b, k)
-            make_forward(p, block)
-            wait_bytes(mirror.at[p, block], diag_recv.at[k])
-            multiply(p, block, mirror[p, block], 2.0, False)
-    share_result(p)
+            make_forward(p, shifted(b, k))
+
+    @each(0, src_count)
+    def _(step):
+        @pl.when(step < p)
+        def _():
+            share_coef(p - 1 - step)
+
+    @each(0, src_count)
+    def _(slot):
+        @pl.when(slot > p)
+        def _():
+            share_coef(slot)
+
+
+    def take_diagonal():
+        for k in range(1, half + 1):
+            @pl.when(diag_target(k))
+            def _():
+                block = shifted(b, k)
+                wait_bytes(mirror.at[p, block], diag_recv.at[k])
+                multiply(p, block, mirror[p, block], 2.0, False)
+        share_result(p)
 
     def source_block(slot, j):
         return jnp.where(slot < p, shifted(b, -offsets[j]), shifted(b, offsets[j]))
 
-    @each(0, src_count)
-    def _(slot):
-        @pl.when(jnp.logical_and(slot != p, count(slot, p) > 0))
+    def prepare(slot):
+        @pl.when(count(slot, p) > 0)
         def _():
             wait_bytes(coef.at[slot, :, pl.ds(0, eigen - piece), :], share_recv.at[slot])
             partial[slot] = jnp.zeros(partial.shape[1:], jnp.float32)
-            for j in range(blocks):
-                @pl.when(goes(slot, p, j))
-                def _():
-                    make_forward(slot, source_block(slot, j))
-
-    def take_unit(slot, j):
-        @pl.when(goes(slot, p, j))
-        def _():
-            block = source_block(slot, j)
-            wait_bytes(mirror.at[slot, block], tile_recv.at[slot, block])
-            multiply(slot, block, mirror[slot, block], 1.0, False)
+            for block in range(blocks):
+                make_forward(slot, block)
+
+    def take_units(slot, start, stop):
+        @pl.when(goes(slot, p, start))
+        def _():
+            for j in range(start, stop):
+                block = source_block(slot, j)
+                wait_bytes(mirror.at[slot, block], tile_recv.at[slot, block])
+            for j in range(start, stop):
+                block = source_block(slot, j)
+                multiply(slot, block, mirror[slot, block], 1.0, False)
 
     def finish(slot):
         @pl.when(count(slot, p) > 0)
@@ -315,35 +324,22 @@
             share_result(slot)
             send_result(slot)
 
-    @pl.when(p > 0)
-    def _():
-        take_unit(p - 1, 0)
-
-    @pl.when(p < last)
-    def _():
-        take_unit(p + 1, half)
-
-    @each(0, src_count)
-    def _(slot):
-        @pl.when(jnp.logical_or(slot > p + 1, slot < p - 1))
-        def _():
-            for j in range(blocks):
-                take_unit(slot, j)
-            finish(slot)
-
-    @pl.when(p > 0)
-    def _():
-        for j in range(1, half):
-            take_unit(p - 1, j)
-        finish(p - 1)
-
-    @pl.when(p < last)
-    def _():
-        for j in range(half + 1, blocks):
-            take_unit(p + 1, j)
-        finish(p + 1)
-
-    wait_bytes(result.at[p, 0, pl.ds(0, blocks - 1)], result_send.at[p])
+    def take_all(slot):
+        take_units(slot, 0, half)
+        take_units(slot, half, blocks)
+        finish(slot)
+
+    @each(0, src_count)
+    def _(slot):
+        @pl.when(slot != p)
+        def _():
+            prepare(slot)
+            take_all(slot)
+
+        @pl.when(slot == jnp.where(p == 0, 1, 0))
+        def _():
+            take_diagonal()
+
     for k in range(1, half + 1):
         @pl.when(diag_source(k))
         def _():
@@ -359,19 +355,14 @@
             def _():
                 wait_bytes(coef.at[slot, :, pl.ds(0, piece), :], coef_send.at[slot])
 
-            @pl.when(sent == half)
-            def _():
-                wait_bytes(mirror.at[slot, pl.ds(0, half)], tile_send.at[slot])
-
-            @pl.when(sent == blocks)
-            def _():
-                wait_bytes(mirror.at[slot], tile_send.at[slot])
+            for n in range(1, blocks + 1):
+                @pl.when(sent == n)
+                def _():
+                    wait_bytes(mirror.at[slot, pl.ds(0, n)], tile_send.at[slot])
 
             @pl.when(received > 0)
             def _():
                 wait_bytes(coef.at[slot, :, pl.ds(0, eigen - piece), :], share_send.at[slot])
-                wait_bytes(result.at[slot, 0], result_send.at[slot])
-                wait_bytes(result.at[slot, 0, pl.ds(0, blocks - 1)], result_send.at[slot])
 
     @each(0, src_count)
     def _(slot):
@@ -395,6 +386,15 @@
             rows[part] = jnp.where(lane == slot, value, rows[part])
     out_ref[0, 0, 0] = rows[0]
     out_ref[0, 1, 0] = rows[1]
+
+    wait_bytes(result.at[p, 0, pl.ds(0, blocks - 1)], result_send.at[p])
+
+    @each(0, src_count)
+    def _(slot):
+        @pl.when(jnp.logical_and(slot != p, count(slot, p) > 0))
+        def _():
+            wait_bytes(result.at[slot, 0], result_send.at[slot])
+            wait_bytes(result.at[slot, 0, pl.ds(0, blocks - 1)], result_send.at[slot])
 
 
 def on_device(sizes, perambulator, elemental, source_order, column_order):
@@ -436,7 +436,6 @@
             sem((slots,)),
             sem((slots, 2)),
             flag((slots,)),
-            flag,
         ],
         compiler_params=pltpu.CompilerParams(collective_id=0, has_side_effects=True),
     )(perambulator, elemental, source_order, column_order)

time: 25.3 us -> 21.8 us (0.86)
  Pallas kernels: 24.6 us -> 21 us
    pallas_call x1, Pallas kernels: 24.6 us -> 21 us  [on_device(): pl.pallas_call(functools.partial(kernel, sizes), out_shape=pltpu.VMEM((1,...]
where the time goes in v3:
time: 21.8 us; the launch traced here: 21.6 us
  Pallas kernels  21 us (96%)
  local copies, waits for them, and re-layouts  0.56 us (3%)
    pallas_call x1, Pallas kernels, on_device(): pl.pallas_call(functools.partial(kernel, sizes), out_shape=pltpu.VMEM((1,...  21 us
    unnamed x1, local copies, waits for them, and re-layouts  0.56 us

profile of v3, /device:TPU:0, one launch (start us, length us, event | category | flops | bytes accessed | tf_op | source)
XLA Modules:
  0.0 21.6 jit_solution(2383885469145852857)
XLA Ops:
  0.0 21.0 %shard_map.46 = f32[1,2,1,1,4]{4,3,2,1,0:T(1,128)S(1)} custom-call(bf16[1,4,2,128,512]{4,3,2,1,0:T(8,128)(2,1)} %tiles_hbm.1, bf16[1,1,2,128,128]{4,3,2,1,0:T(8,128)(2,1)} %elem_hbm.1, s32[4]{0:T(128)} %order_hbm.1, s32[1,128]{1,0:T(1,128)} %column_hbm.1), custom_call_target="tpu_custom_call" | custom-call | tf_op jit(solution)/shard_map/pallas_call | solution.py:409
  21.0 0.6 %copy.6 = f32[1,2,1,1,4]{4,3,2,1,0:T(1,128)} copy(f32[1,2,1,1,4]{4,3,2,1,0:T(1,128)S(1)} %shard_map.46) | data formatting | bytes 64

commit v4 on v3

--- a/solution.py
+++ b/solution.py
@@ -22,8 +22,7 @@
     out_ref,
     tiles, elem, order, column,
     near, coef, left, mirror, forward, partial, result, total,
-    load_sem, tile_send, tile_recv, coef_send, coef_recv, share_send, share_recv,
-    diag_send, diag_recv, result_send, result_recv, above,
+    gone, tile_recv, coef_recv, share_recv, result_recv, above,
 ):
     src_count, col_count, half_count = sizes
     blocks = col_count * half_count
@@ -48,9 +47,9 @@
     def signal(sem, slot, block):
         pl.semaphore_signal(sem, inc=1, device_id=device(slot, block), device_id_type=MESH)
 
-    def send(src, dst, send_sem, recv_sem, slot, block):
+    def send(src, dst, recv_sem, slot, block):
         pltpu.make_async_remote_copy(
-            src_ref=src, dst_ref=dst, send_sem=send_sem, recv_sem=recv_sem,
+            src_ref=src, dst_ref=dst, send_sem=gone, recv_sem=recv_sem,
             device_id=device(slot, block), device_id_type=MESH,
         ).start()
 
@@ -75,7 +74,7 @@
 
     def upward(low, high):
         whole = jnp.where(jnp.logical_or(lax.rem(high, 2) == 0, high - low == 1), blocks, 0)
-        return jnp.where(high == 1, half, whole)
+        return jnp.where(high == 1, 1, whole)
 
     def count(source, target):
         n = upward(jnp.minimum(source, target), jnp.maximum(source, target))
@@ -98,10 +97,10 @@
                 signal(barrier, slot, k)
 
     loads = [
-        pltpu.make_async_copy(elem_hbm.at[0, 0], elem, load_sem.at[0]),
-        pltpu.make_async_copy(column_hbm, column, load_sem.at[1]),
-        pltpu.make_async_copy(order_hbm, order, load_sem.at[2]),
-        pltpu.make_async_copy(tiles_hbm.at[0], tiles, load_sem.at[3]),
+        pltpu.make_async_copy(elem_hbm.at[0, 0], elem, coef_recv.at[p]),
+        pltpu.make_async_copy(column_hbm, column, share_recv.at[p]),
+        pltpu.make_async_copy(order_hbm, order, tile_recv.at[p, 1]),
+        pltpu.make_async_copy(tiles_hbm.at[0], tiles, tile_recv.at[p, 2]),
     ]
     for load in loads:
         load.start()
@@ -127,8 +126,7 @@
     loads[2].wait()
     loads[3].wait()
 
-    @each(0, src_count)
-    def _(slot):
+    def sort(slot):
         for spin in range(spins):
             near[slot, spin] = tiles[order[slot], :, :, spin * eigen : (spin + 1) * eigen]
 
@@ -139,17 +137,24 @@
         def _():
             send(
                 coef.at[p, :, my_piece, :], coef.at[p, :, my_piece, :],
-                coef_send.at[slot], coef_recv.at[p], slot, b,
+                coef_recv.at[p], slot, b,
             )
+
+    groups = [(0, 1), (1, half), (half, blocks)]
+
+    def group_of(j):
+        return [start <= j < stop for start, stop in groups].index(True)
+
+    def offset_of(j):
+        return jnp.where(lax.rem(b, 2) == 0, offsets[j], offsets[j ^ 1])
 
     def send_unit(slot, j):
         @pl.when(goes(p, slot, j))
         def _():
-            offset = jnp.where(lax.rem(b, 2) == 0, offsets[j], offsets[j ^ 1])
-            block = jnp.where(p < slot, shifted(b, offset), shifted(b, -offset))
+            block = jnp.where(p < slot, shifted(b, offset_of(j)), shifted(b, -offset_of(j)))
             send(
                 near.at[slot, spin_of(block)], mirror.at[p, b],
-                tile_send.at[slot], tile_recv.at[p, b], slot, block,
+                tile_recv.at[p, group_of(j)], slot, block,
             )
 
     def send_units(slot, start, stop):
@@ -166,7 +171,14 @@
     def _(slot):
         @pl.when(slot < p)
         def _():
+            sort(slot)
             send_units(slot, 0, blocks)
+
+    @each(0, src_count)
+    def _(slot):
+        @pl.when(slot >= p)
+        def _():
+            sort(slot)
 
     @pl.when(p < last)
     def _():
@@ -200,7 +212,7 @@
             for k in range(1, blocks):
                 send(
                     coef.at[slot, :, my_piece, :], coef.at[slot, :, my_piece, :],
-                    share_send.at[slot], share_recv.at[slot], p, shifted(b, k),
+                    share_recv.at[slot], p, shifted(b, k),
                 )
 
     def diag_source(k):
@@ -215,7 +227,7 @@
             block = shifted(b, -k)
             send(
                 near.at[p, spin_of(block)], mirror.at[p, b],
-                diag_send.at[k], diag_recv.at[k], p, block,
+                tile_recv.at[p, 0], p, block,
             )
 
     own_real, own_imag = coef[p, 0, rows_of(b), :], coef[p, 1, rows_of(b), :]
@@ -252,20 +264,20 @@
             partial[slot] += packed
 
     def share_result(slot):
-        result[slot, 0, b] = partial[slot]
+        result[slot, b] = partial[slot]
         for k in range(1, blocks):
             block = shifted(b, k)
             send(
-                result.at[slot, 0, b], result.at[slot, 0, b],
-                result_send.at[slot], result_recv.at[slot, 0], p, block,
+                result.at[slot, b], result.at[slot, b],
+                result_recv.at[slot], p, block,
             )
 
     def send_result(slot):
         for k in range(blocks):
             block = shifted(b, k)
             send(
-                result.at[slot, 0, b], result.at[p, 1, b],
-                result_send.at[slot], result_recv.at[p, 1], slot, block,
+                result.at[slot, b], result.at[p, blocks + b],
+                result_recv.at[p], slot, block,
             )
 
     make_forward(p, b)
@@ -289,16 +301,20 @@
 
 
     def take_diagonal():
+        for n in (half - 1, half):
+            @pl.when(diag_target(half) == (n == half))
+            def _():
+                wait_bytes(mirror.at[p, pl.ds(0, n)], tile_recv.at[p, 0])
+
         for k in range(1, half + 1):
             @pl.when(diag_target(k))
             def _():
                 block = shifted(b, k)
-                wait_bytes(mirror.at[p, block], diag_recv.at[k])
                 multiply(p, block, mirror[p, block], 2.0, False)
         share_result(p)
 
     def source_block(slot, j):
-        return jnp.where(slot < p, shifted(b, -offsets[j]), shifted(b, offsets[j]))
+        return jnp.where(slot < p, shifted(b, -offset_of(j)), shifted(b, offset_of(j)))
 
     def prepare(slot):
         @pl.when(count(slot, p) > 0)
@@ -311,9 +327,7 @@
     def take_units(slot, start, stop):
         @pl.when(goes(slot, p, start))
         def _():
-            for j in range(start, stop):
-                block = source_block(slot, j)
-                wait_bytes(mirror.at[slot, block], tile_recv.at[slot, block])
+            wait_bytes(mirror.at[slot, pl.ds(0, stop - start)], tile_recv.at[slot, group_of(start)])
             for j in range(start, stop):
                 block = source_block(slot, j)
                 multiply(slot, block, mirror[slot, block], 1.0, False)
@@ -325,8 +339,8 @@
             send_result(slot)
 
     def take_all(slot):
-        take_units(slot, 0, half)
-        take_units(slot, half, blocks)
+        for start, stop in groups:
+            take_units(slot, start, stop)
         finish(slot)
 
     @each(0, src_count)
@@ -343,7 +357,7 @@
     for k in range(1, half + 1):
         @pl.when(diag_source(k))
         def _():
-            wait_bytes(mirror.at[p, 0], diag_send.at[k])
+            wait_bytes(mirror.at[p, 0], gone)
 
     @each(0, src_count)
     def _(slot):
@@ -353,16 +367,26 @@
 
             @pl.when(sent > 0)
             def _():
-                wait_bytes(coef.at[slot, :, pl.ds(0, piece), :], coef_send.at[slot])
+                wait_bytes(coef.at[slot, :, pl.ds(0, piece), :], gone)
 
             for n in range(1, blocks + 1):
                 @pl.when(sent == n)
                 def _():
-                    wait_bytes(mirror.at[slot, pl.ds(0, n)], tile_send.at[slot])
+                    wait_bytes(mirror.at[slot, pl.ds(0, n)], gone)
 
             @pl.when(received > 0)
             def _():
-                wait_bytes(coef.at[slot, :, pl.ds(0, eigen - piece), :], share_send.at[slot])
+                wait_bytes(coef.at[slot, :, pl.ds(0, eigen - piece), :], gone)
+
+    @each(0, src_count)
+    def _(slot):
+        here = jnp.logical_or(slot == p, count(slot, p) > 0)
+        there = jnp.logical_and(slot != p, count(p, slot) > 0)
+        expected = jnp.where(here, blocks - 1, 0) + jnp.where(there, blocks, 0)
+        for n in (blocks - 1, blocks, 2 * blocks - 1):
+            @pl.when(expected == n)
+            def _():
+                wait_bytes(result.at[slot, pl.ds(0, n)], result_recv.at[slot])
 
     @each(0, src_count)
     def _(slot):
@@ -370,31 +394,35 @@
 
         @pl.when(jnp.logical_or(slot == p, count(slot, p) > 0))
         def _():
-            wait_bytes(result.at[slot, 0, pl.ds(0, blocks - 1)], result_recv.at[slot, 0])
-            total[slot] += jnp.sum(result[slot, 0], axis=0)
+            total[slot] += jnp.sum(result[slot, :blocks], axis=0)
 
         @pl.when(jnp.logical_and(slot != p, count(p, slot) > 0))
         def _():
-            wait_bytes(result.at[slot, 1], result_recv.at[slot, 1])
-            total[slot] += jnp.sum(result[slot, 1], axis=0)
-
-    lane = lax.broadcasted_iota(jnp.int32, (1, src_count), 1)
-    rows = [jnp.zeros((1, src_count), jnp.float32)] * 2
-    for slot in range(src_count):
-        for part in (0, 1):
-            value = jnp.sum(total[slot, 4 * part : 4 * part + 4], keepdims=True)
-            rows[part] = jnp.where(lane == slot, value, rows[part])
-    out_ref[0, 0, 0] = rows[0]
-    out_ref[0, 1, 0] = rows[1]
-
-    wait_bytes(result.at[p, 0, pl.ds(0, blocks - 1)], result_send.at[p])
+            total[slot] += jnp.sum(result[slot, blocks:], axis=0)
+
+    rows = jnp.concatenate(
+        [
+            jnp.sum(total[slot, 4 * part : 4 * part + 4], axis=0, keepdims=True)
+            for part in (0, 1)
+            for slot in range(src_count)
+        ],
+        axis=0,
+    )
+    sums = jnp.sum(rows, axis=1, keepdims=True)
+    lane = lax.broadcasted_iota(jnp.int32, (src_count, src_count), 1)
+    row = lax.broadcasted_iota(jnp.int32, (src_count, src_count), 0)
+    for part in (0, 1):
+        picked = jnp.where(lane == row, sums[part * src_count : (part + 1) * src_count], 0.0)
+        out_ref[0, part, 0] = jnp.sum(picked, axis=0, keepdims=True)
+
+    wait_bytes(result.at[p, pl.ds(0, blocks - 1)], gone)
 
     @each(0, src_count)
     def _(slot):
         @pl.when(jnp.logical_and(slot != p, count(slot, p) > 0))
         def _():
-            wait_bytes(result.at[slot, 0], result_send.at[slot])
-            wait_bytes(result.at[slot, 0, pl.ds(0, blocks - 1)], result_send.at[slot])
+            wait_bytes(result.at[slot, pl.ds(0, blocks)], gone)
+            wait_bytes(result.at[slot, pl.ds(0, blocks - 1)], gone)
 
 
 def on_device(sizes, perambulator, elemental, source_order, column_order):
@@ -422,19 +450,13 @@
             pltpu.VMEM((slots, blocks, 2, block_cols, eigen), jnp.bfloat16),
             pltpu.VMEM((slots, blocks, 2, block_cols, block_cols), jnp.bfloat16),
             pltpu.VMEM((slots, 8, block_cols), jnp.float32),
-            pltpu.VMEM((slots, 2, blocks, 8, block_cols), jnp.float32),
+            pltpu.VMEM((slots, 2 * blocks, 8, block_cols), jnp.float32),
             pltpu.VMEM((slots, 8, block_cols), jnp.float32),
-            sem((4,)),
-            sem((slots,)),
-            sem((slots, blocks)),
+            sem,
+            sem((slots, 3)),
             sem((slots,)),
             sem((slots,)),
             sem((slots,)),
-            sem((slots,)),
-            sem((blocks,)),
-            sem((blocks,)),
-            sem((slots,)),
-            sem((slots, 2)),
             flag((slots,)),
         ],
         compiler_params=pltpu.CompilerParams(collective_id=0, has_side_effects=True),

time: 21.8 us -> 21.3 us (0.977)
  Pallas kernels: 21 us -> 20.6 us
    pallas_call x1, Pallas kernels: 21 us -> 20.6 us  [on_device(): pl.pallas_call(functools.partial(kernel, sizes), out_shape=pltpu.VMEM((1,...]
where the time goes in v4:
time: 21.3 us; the launch traced here: 21.1 us
  Pallas kernels  20.6 us (97%)
  local copies, waits for them, and re-layouts  0.56 us (3%)
    pallas_call x1, Pallas kernels, on_device(): pl.pallas_call(functools.partial(kernel, sizes), out_shape=pltpu.VMEM((1,...  20.6 us
    unnamed x1, local copies, waits for them, and re-layouts  0.56 us

profile of v4, /device:TPU:0, one launch (start us, length us, event | category | flops | bytes accessed | tf_op | source)
XLA Modules:
  0.0 21.1 jit_solution(14119086489250791498)
XLA Ops:
  0.0 20.6 %shard_map.46 = f32[1,2,1,1,4]{4,3,2,1,0:T(1,128)S(1)} custom-call(bf16[1,4,2,128,512]{4,3,2,1,0:T(8,128)(2,1)} %tiles_hbm.1, bf16[1,1,2,128,128]{4,3,2,1,0:T(8,128)(2,1)} %elem_hbm.1, s32[4]{0:T(128)} %order_hbm.1, s32[1,128]{1,0:T(1,128)} %column_hbm.1), custom_call_target="tpu_custom_call" | custom-call | tf_op jit(solution)/shard_map/pallas_call | solution.py:437
  20.6 0.6 %copy.6 = f32[1,2,1,1,4]{4,3,2,1,0:T(1,128)} copy(f32[1,2,1,1,4]{4,3,2,1,0:T(1,128)S(1)} %shard_map.46) | data formatting | bytes 64

commit v5 on v4

--- a/solution.py
+++ b/solution.py
@@ -74,7 +74,7 @@
 
     def upward(low, high):
         whole = jnp.where(jnp.logical_or(lax.rem(high, 2) == 0, high - low == 1), blocks, 0)
-        return jnp.where(high == 1, 1, whole)
+        return jnp.where(high == 1, half, whole)
 
     def count(source, target):
         n = upward(jnp.minimum(source, target), jnp.maximum(source, target))
@@ -99,19 +99,24 @@
     loads = [
         pltpu.make_async_copy(elem_hbm.at[0, 0], elem, coef_recv.at[p]),
         pltpu.make_async_copy(column_hbm, column, share_recv.at[p]),
-        pltpu.make_async_copy(order_hbm, order, tile_recv.at[p, 1]),
-        pltpu.make_async_copy(tiles_hbm.at[0], tiles, tile_recv.at[p, 2]),
+        pltpu.make_async_copy(order_hbm, order, tile_recv.at[p, 2]),
+        pltpu.make_async_copy(tiles_hbm.at[0], tiles, tile_recv.at[p, 1]),
     ]
     for load in loads:
         load.start()
 
-    pl.semaphore_wait(barrier, blocks - 1 + p * blocks)
-
-    @each(0, src_count)
-    def _(slot):
-        @pl.when(slot < p)
-        def _():
-            signal(above.at[p], slot, b)
+    first_column = b < half_count
+
+    def greet():
+        pl.semaphore_wait(barrier, blocks - 1 + p * blocks)
+
+        @each(0, src_count)
+        def _(slot):
+            @pl.when(slot < p)
+            def _():
+                signal(above.at[p], slot, b)
+
+    pl.when(jnp.logical_not(first_column))(greet)
 
     loads[0].wait()
     loads[1].wait()
@@ -125,6 +130,7 @@
 
     loads[2].wait()
     loads[3].wait()
+    pl.when(first_column)(greet)
 
     def sort(slot):
         for spin in range(spins):
@@ -140,13 +146,13 @@
                 coef_recv.at[p], slot, b,
             )
 
-    groups = [(0, 1), (1, half), (half, blocks)]
+    groups = [(0, half), (half, blocks - 1), (blocks - 1, blocks)]
 
     def group_of(j):
         return [start <= j < stop for start, stop in groups].index(True)
 
     def offset_of(j):
-        return jnp.where(lax.rem(b, 2) == 0, offsets[j], offsets[j ^ 1])
+        return offsets[j]
 
     def send_unit(slot, j):
         @pl.when(goes(p, slot, j))
@@ -186,6 +192,11 @@
         send_coef(p + 1)
         send_units(p + 1, 0, 1)
 
+        @pl.when(p == 0)
+        def _():
+            send_units(p + 1, 1, blocks)
+
+
     @each(0, src_count)
     def _(slot):
         @pl.when(slot > p + 1)
@@ -194,7 +205,7 @@
             send_coef(slot)
             send_units(slot, 0, blocks)
 
-    @pl.when(p < last)
+    @pl.when(jnp.logical_and(p > 0, p < last))
     def _():
         send_units(p + 1, 1, blocks)
 
@@ -388,8 +399,6 @@
             def _():
                 wait_bytes(result.at[slot, pl.ds(0, n)], result_recv.at[slot])
 
-    @each(0, src_count)
-    def _(slot):
         total[slot] = jnp.zeros(total.shape[1:], jnp.float32)
 
         @pl.when(jnp.logical_or(slot == p, count(slot, p) > 0))

time: 21.3 us -> 21.3 us (level)
  no operation moved by 1% of the time
where the time goes in v5:
time: 21.3 us; the launch traced here: 21.1 us
  Pallas kernels  20.5 us (96%)
  local copies, waits for them, and re-layouts  0.56 us (3%)
    pallas_call x1, Pallas kernels, on_device(): pl.pallas_call(functools.partial(kernel, sizes), out_shape=pltpu.VMEM((1,...  20.5 us
    unnamed x1, local copies, waits for them, and re-layouts  0.56 us

profile of v5, /device:TPU:0, one launch (start us, length us, event | category | flops | bytes accessed | tf_op | source)
XLA Modules:
  0.0 21.1 jit_solution(2747512541579731682)
XLA Ops:
  0.0 20.5 %shard_map.46 = f32[1,2,1,1,4]{4,3,2,1,0:T(1,128)S(1)} custom-call(bf16[1,4,2,128,512]{4,3,2,1,0:T(8,128)(2,1)} %tiles_hbm.1, bf16[1,1,2,128,128]{4,3,2,1,0:T(8,128)(2,1)} %elem_hbm.1, s32[4]{0:T(128)} %order_hbm.1, s32[1,128]{1,0:T(1,128)} %column_hbm.1), custom_call_target="tpu_custom_call" | custom-call | tf_op jit(solution)/shard_map/pallas_call | solution.py:446
  20.6 0.6 %copy.6 = f32[1,2,1,1,4]{4,3,2,1,0:T(1,128)} copy(f32[1,2,1,1,4]{4,3,2,1,0:T(1,128)S(1)} %shard_map.46) | data formatting | bytes 64

commit v6 on v5

--- a/solution.py
+++ b/solution.py
@@ -138,8 +138,11 @@
 
     my_piece = pl.ds(pl.multiple_of(b * piece, piece), piece)
 
+    def relayed(source, target):
+        return (target == 0) & (source > 1) & (count(source, 1) > 0)
+
     def send_coef(slot):
-        @pl.when(count(p, slot) > 0)
+        @pl.when((count(p, slot) > 0) & jnp.logical_not(relayed(p, slot)))
         def _():
             send(
                 coef.at[p, :, my_piece, :], coef.at[p, :, my_piece, :],
@@ -178,7 +181,13 @@
         @pl.when(slot < p)
         def _():
             sort(slot)
-            send_units(slot, 0, blocks)
+            send_units(slot, 0, half)
+
+    @each(0, src_count)
+    def _(slot):
+        @pl.when(slot < p)
+        def _():
+            send_units(slot, half, blocks)
 
     @each(0, src_count)
     def _(slot):
@@ -220,6 +229,14 @@
         @pl.when(count(slot, p) > 0)
         def _():
             wait_bytes(coef.at[slot, :, pl.ds(0, piece), :], coef_recv.at[slot])
+
+            @pl.when((p == 1) & (count(slot, 0) > 0) & relayed(slot, 0))
+            def _():
+                send(
+                    coef.at[slot, :, my_piece, :], coef.at[slot, :, my_piece, :],
+                    coef_recv.at[slot], 0, b,
+                )
+
             for k in range(1, blocks):
                 send(
                     coef.at[slot, :, my_piece, :], coef.at[slot, :, my_piece, :],
@@ -274,21 +291,22 @@
         else:
             partial[slot] += packed
 
+    def by_column(j):
+        return jnp.where(lax.rem(b, 2) == 0, j, j ^ 1)
+
     def share_result(slot):
-        result[slot, b] = partial[slot]
-        for k in range(1, blocks):
-            block = shifted(b, k)
-            send(
-                result.at[slot, b], result.at[slot, b],
-                result_recv.at[slot], p, block,
-            )
+        for j in range(blocks):
+            block = by_column(j)
+
+            @pl.when(block != b)
+            def _():
+                send(result.at[slot, b], result.at[slot, b], result_recv.at[slot], p, block)
 
     def send_result(slot):
-        for k in range(blocks):
-            block = shifted(b, k)
+        for j in range(blocks):
             send(
                 result.at[slot, b], result.at[p, blocks + b],
-                result_recv.at[p], slot, block,
+                result_recv.at[p], slot, by_column(j),
             )
 
     make_forward(p, b)
@@ -322,6 +340,7 @@
             def _():
                 block = shifted(b, k)
                 multiply(p, block, mirror[p, block], 2.0, False)
+        result[p, b] = partial[p]
         share_result(p)
 
     def source_block(slot, j):
@@ -346,8 +365,17 @@
     def finish(slot):
         @pl.when(count(slot, p) > 0)
         def _():
+            result[slot, b] = partial[slot]
+
+            @pl.when(slot < p)
+            def _():
+                send_result(slot)
+
             share_result(slot)
-            send_result(slot)
+
+            @pl.when(slot > p)
+            def _():
+                send_result(slot)
 
     def take_all(slot):
         for start, stop in groups:
@@ -376,7 +404,11 @@
         def _():
             sent, received = count(p, slot), count(slot, p)
 
-            @pl.when(sent > 0)
+            @pl.when((sent > 0) & jnp.logical_not(relayed(p, slot)))
+            def _():
+                wait_bytes(coef.at[slot, :, pl.ds(0, piece), :], gone)
+
+            @pl.when((p == 1) & (received > 0) & (count(slot, 0) > 0) & relayed(slot, 0))
             def _():
                 wait_bytes(coef.at[slot, :, pl.ds(0, piece), :], gone)
 

time: 21.3 us -> 21 us (0.986)
    pallas_call x1, Pallas kernels: 20.5 us -> 20.3 us  [on_device(): pl.pallas_call(functools.partial(kernel, sizes), out_shape=pltpu.VMEM((1,...]
where the time goes in v6:
time: 21 us; the launch traced here: 20.9 us
  Pallas kernels  20.3 us (97%)
  local copies, waits for them, and re-layouts  0.56 us (3%)
    pallas_call x1, Pallas kernels, on_device(): pl.pallas_call(functools.partial(kernel, sizes), out_shape=pltpu.VMEM((1,...  20.3 us
    unnamed x1, local copies, waits for them, and re-layouts  0.56 us

profile of v6, /device:TPU:0, one launch (start us, length us, event | category | flops | bytes accessed | tf_op | source)
XLA Modules:
  0.0 20.9 jit_solution(7243020061996456404)
XLA Ops:
  0.0 20.3 %shard_map.46 = f32[1,2,1,1,4]{4,3,2,1,0:T(1,128)S(1)} custom-call(bf16[1,4,2,128,512]{4,3,2,1,0:T(8,128)(2,1)} %tiles_hbm.1, bf16[1,1,2,128,128]{4,3,2,1,0:T(8,128)(2,1)} %elem_hbm.1, s32[4]{0:T(128)} %order_hbm.1, s32[1,128]{1,0:T(1,128)} %column_hbm.1), custom_call_target="tpu_custom_call" | custom-call | tf_op jit(solution)/shard_map/pallas_call | solution.py:478
  20.3 0.6 %copy.6 = f32[1,2,1,1,4]{4,3,2,1,0:T(1,128)} copy(f32[1,2,1,1,4]{4,3,2,1,0:T(1,128)S(1)} %shard_map.46) | data formatting | bytes 64

commit v7 on v6

--- a/solution.py
+++ b/solution.py
@@ -181,13 +181,14 @@
         @pl.when(slot < p)
         def _():
             sort(slot)
-            send_units(slot, 0, half)
-
-    @each(0, src_count)
-    def _(slot):
-        @pl.when(slot < p)
-        def _():
-            send_units(slot, half, blocks)
+            send_units(slot, 0, 1)
+
+    for j in range(1, blocks):
+        @each(0, src_count)
+        def _(slot):
+            @pl.when(slot < p)
+            def _():
+                send_units(slot, j, j + 1)
 
     @each(0, src_count)
     def _(slot):

time: 21 us -> 21.7 us (1.033)
  Pallas kernels: 20.3 us -> 20.9 us
    pallas_call x1, Pallas kernels: 20.3 us -> 20.9 us  [on_device(): pl.pallas_call(functools.partial(kernel, sizes), out_shape=pltpu.VMEM((1,...]
where the time goes in v7:
time: 21.7 us; the launch traced here: 21.5 us
  Pallas kernels  20.9 us (96%)
  local copies, waits for them, and re-layouts  0.56 us (3%)
    pallas_call x1, Pallas kernels, on_device(): pl.pallas_call(functools.partial(kernel, sizes), out_shape=pltpu.VMEM((1,...  20.9 us
    unnamed x1, local copies, waits for them, and re-layouts  0.56 us

profile of v7, /device:TPU:0, one launch (start us, length us, event | category | flops | bytes accessed | tf_op | source)
XLA Modules:
  0.0 21.5 jit_solution(579690027431021423)
XLA Ops:
  0.0 20.9 %shard_map.46 = f32[1,2,1,1,4]{4,3,2,1,0:T(1,128)S(1)} custom-call(bf16[1,4,2,128,512]{4,3,2,1,0:T(8,128)(2,1)} %tiles_hbm.1, bf16[1,1,2,128,128]{4,3,2,1,0:T(8,128)(2,1)} %elem_hbm.1, s32[4]{0:T(128)} %order_hbm.1, s32[1,128]{1,0:T(1,128)} %column_hbm.1), custom_call_target="tpu_custom_call" | custom-call | tf_op jit(solution)/shard_map/pallas_call | solution.py:479
  20.9 0.6 %copy.6 = f32[1,2,1,1,4]{4,3,2,1,0:T(1,128)} copy(f32[1,2,1,1,4]{4,3,2,1,0:T(1,128)S(1)} %shard_map.46) | data formatting | bytes 64
